TPU v7x, 128 devices: a whole 4x4x4 slice. The times are simulated.
128 devices in a mesh: shard: 16 (over z, x), context: 4 (over y), tensor: 2 (over core).
Axes of the slice: x: 4, y: 4, z: 4, core: 2. Of those that a mesh axis runs over, the one named last changes fastest.
Arguments:
- inputs: float32 [32, 512, 768], P('shard', 'context'), may hold values from -6 to 6
- segment_ids: int32 [32, 512], P('shard', 'context'), may hold values from 0 to 3, never falling along the last dimension, each value on 1 to 256 neighbouring positions
- projection: bfloat16 [2, 3, 768, 768], P(None, None, 'shard', 'tensor'), may hold values from -1 to 1
- head_bias: bfloat16 [2, 2, 12, 64], P(None, None, 'tensor', 'shard'), may hold values from -3 to 3
- mixing: bfloat16 [2, 768, 768], P(None, 'tensor', 'shard'), may hold values from -0.875 to 0.875
- expansion: bfloat16 [2, 768, 3072], P(None, 'shard', 'tensor'), may hold values from -0.21875 to 0.21875
- hidden_bias: bfloat16 [2, 48, 64], P(None, 'tensor', 'shard'), may hold values from -3 to 3
- contraction: bfloat16 [2, 3072, 768], P(None, 'tensor', 'shard'), may hold values from -0.109375 to 0.109375
- norm_gains: bfloat16 [2, 2, 768], P(None, None, 'shard'), may hold values from 0.3984375 to 1.59375
- offsets: bfloat16 [2, 4, 768], P(None, None, 'shard'), may hold values from -2 to 2
- cotangent: float32 [32, 512, 768], P('shard', 'context'), may hold values from -6 to 6
Outputs:
- outputs: float32 [32, 512, 768], P('shard', 'context')
- input_grad: float32 [32, 512, 768], P('shard', 'context')
- grad_projection: float32 [2, 3, 768, 768], P(None, None, 'shard', 'tensor')
- head_grad: float32 [2, 2, 12, 64], P(None, None, 'tensor', 'shard')
- grad_mixing: float32 [2, 768, 768], P(None, 'tensor', 'shard')
- grad_expansion: float32 [2, 768, 3072], P(None, 'shard', 'tensor')
- hidden_grad: float32 [2, 48, 64], P(None, 'tensor', 'shard')
- grad_contraction: float32 [2, 3072, 768], P(None, 'tensor', 'shard')
- gains_grad: float32 [2, 2, 768], P(None, None, 'shard')
- grad_offsets: float32 [2, 4, 768], P(None, None, 'shard')
Inputs may be any that keep to these rules, and one draw needn't show every extreme that they name: `segment_ids`: within a row ids never fall; every document holds 1 to 256 positions and in every row some document holds exactly 256.
All inputs are finite; a program needn't handle non-finite values.
Results may differ from a plain program's by a relative error of at most 0.033.
Values may be sent and summed in bfloat16 or wider, within the bound.
No kernel may reach another device: no remote copies, remote signals or barrier semaphores. Data moves between devices by JAX's collectives and lax.ppermute only.
A program may use at most 128 MiB of HBM per device.

v0:
```python
import jax
import jax.numpy as jnp
from jax import lax
from jax.sharding import PartitionSpec as P

HEAD = 64


EPS = 1e-05
GELU_COEF = 0.7978845608028654
GELU_CUBE = 0.044715
MASKED = -1e30


def gelu_value(preact):
    inner_arg = GELU_COEF * (preact + GELU_CUBE * preact * preact * preact)
    return 0.5 * preact * (1.0 + jnp.tanh(inner_arg))


def gelu_slope(preact):
    inner_arg = GELU_COEF * (preact + GELU_CUBE * preact * preact * preact)
    tanh_value = jnp.tanh(inner_arg)
    return 0.5 * (1.0 + tanh_value) + 0.5 * preact * (1.0 - tanh_value * tanh_value) * GELU_COEF * (
        1.0 + 3.0 * GELU_CUBE * preact * preact
    )


def norm_forward(stream):
    center = stream - jnp.mean(stream, axis=-1, keepdims=True)
    spread = lax.rsqrt(jnp.mean(center * center, axis=-1, keepdims=True) + EPS)
    return (center * spread, spread)


def norm_backward(upstream, normed, spread, gain_row):
    scaled = upstream * gain_row
    first_mean = jnp.mean(scaled, axis=-1, keepdims=True)
    second_mean = jnp.mean(scaled * normed, axis=-1, keepdims=True)
    return spread * (scaled - first_mean - normed * second_mean)


def masked_scores(query_block, key_block, visible, head_scale):
    scores = (
        jnp.einsum("rqhe,rkhe->rhqk", query_block, key_block, preferred_element_type=jnp.float32)
        * head_scale
    )
    return jnp.where(visible, scores, MASKED)


def per_device(
    inputs,
    segment_ids,
    projection,
    head_bias,
    mixing,
    expansion,
    hidden_bias,
    contraction,
    norm_gains,
    offsets,
    cotangent,
):
    layers = projection.shape[0]
    row_count, block_length, model_width = inputs.shape
    context_size = lax.axis_size("context")
    heads_here = head_bias.shape[2]
    head_scale = HEAD ** (-0.5)
    segment_half = segment_ids.astype(jnp.bfloat16)
    query_pos = lax.axis_index("context") * block_length + jnp.arange(block_length, dtype=jnp.int32)
    key_pos = jnp.arange(block_length * context_size, dtype=jnp.int32)
    stream = inputs
    kept_state = []
    for layer_index in range(layers):
        weights = (
            lax.all_gather(projection[layer_index], "shard", axis=1, tiled=True),
            lax.all_gather(head_bias[layer_index], "shard", axis=2, tiled=True),
            lax.all_gather(mixing[layer_index], "shard", axis=1, tiled=True),
            lax.all_gather(expansion[layer_index], "shard", axis=0, tiled=True),
            lax.all_gather(hidden_bias[layer_index], "shard", axis=1, tiled=True),
            lax.all_gather(contraction[layer_index], "shard", axis=1, tiled=True),
            lax.all_gather(norm_gains[layer_index], "shard", axis=1, tiled=True),
            lax.all_gather(offsets[layer_index], "shard", axis=1, tiled=True),
        )
        (
            qkv_weight,
            qkv_bias,
            out_weight,
            up_weight,
            up_bias,
            down_weight,
            gain_rows,
            offset_rows,
        ) = weights
        gain_float = gain_rows.astype(jnp.float32)
        offset_float = offset_rows.astype(jnp.float32)
        normed_one, spread_one = norm_forward(stream)
        attend_input = (normed_one * gain_float[0] + offset_float[0]).astype(jnp.bfloat16)
        projected = jnp.einsum(
            "rtd,jdc->jrtc", attend_input, qkv_weight, preferred_element_type=jnp.float32
        )
        bias_float = qkv_bias.astype(jnp.float32).reshape(2, -1)
        query_rows = (projected[0] + bias_float[0]).astype(jnp.bfloat16)
        key_rows = projected[1].astype(jnp.bfloat16)
        value_rows = (projected[2] + bias_float[1]).astype(jnp.bfloat16)
        keys_all, values_all, segments_all = (
            lax.all_gather(key_rows, "context", axis=1, tiled=True),
            lax.all_gather(value_rows, "context", axis=1, tiled=True),
            lax.all_gather(segment_half, "context", axis=1, tiled=True),
        )
        visible = (segments_all[:, None, :] == segment_half[:, :, None]) & (
            key_pos[None, None, :] <= query_pos[None, :, None]
        )
        visible = visible[:, None]
        query_block = query_rows.reshape(row_count, block_length, heads_here, HEAD)
        key_block = keys_all.reshape(row_count, -1, heads_here, HEAD)
        value_block = values_all.reshape(row_count, -1, heads_here, HEAD)
        masked = masked_scores(query_block, key_block, visible, head_scale)
        row_top = jnp.max(masked, axis=-1, keepdims=True)
        log_total = row_top + jnp.log(jnp.sum(jnp.exp(masked - row_top), axis=-1, keepdims=True))
        soft_half = jnp.exp(masked - log_total).astype(jnp.bfloat16)
        attended = (
            jnp.einsum(
                "rhqk,rkhe->rqhe", soft_half, value_block, preferred_element_type=jnp.float32
            )
            .astype(jnp.bfloat16)
            .reshape(row_count, block_length, -1)
        )
        attend_part = jnp.einsum(
            "rtc,cd->rtd", attended, out_weight, preferred_element_type=jnp.float32
        )
        middle = stream + lax.psum(attend_part, "tensor") + offset_float[2]
        normed_two, spread_two = norm_forward(middle)
        feed_input = (normed_two * gain_float[1] + offset_float[1]).astype(jnp.bfloat16)
        preact = jnp.einsum(
            "rtd,df->rtf", feed_input, up_weight, preferred_element_type=jnp.float32
        ) + up_bias.astype(jnp.float32).reshape(-1)
        activation = gelu_value(preact).astype(jnp.bfloat16)
        feed_part = jnp.einsum(
            "rtf,fd->rtd", activation, down_weight, preferred_element_type=jnp.float32
        )
        stream = middle + lax.psum(feed_part, "tensor") + offset_float[3]
        stored = ()
        kept_state.append(
            (
                stored,
                normed_one,
                spread_one,
                attend_input,
                query_block,
                key_block,
                value_block,
                visible,
                log_total,
                attended,
                normed_two,
                spread_two,
                feed_input,
                preact,
                activation,
            )
        )
    upstream = cotangent
    collected = []
    for layer_index in reversed(range(layers)):
        (
            stored,
            normed_one,
            spread_one,
            attend_input,
            query_block,
            key_block,
            value_block,
            visible,
            log_total,
            attended,
            normed_two,
            spread_two,
            feed_input,
            preact,
            activation,
        ) = kept_state[layer_index]
        current = (
            lax.all_gather(projection[layer_index], "shard", axis=1, tiled=True),
            lax.all_gather(head_bias[layer_index], "shard", axis=2, tiled=True),
            lax.all_gather(mixing[layer_index], "shard", axis=1, tiled=True),
            lax.all_gather(expansion[layer_index], "shard", axis=0, tiled=True),
            lax.all_gather(hidden_bias[layer_index], "shard", axis=1, tiled=True),
            lax.all_gather(contraction[layer_index], "shard", axis=1, tiled=True),
            lax.all_gather(norm_gains[layer_index], "shard", axis=1, tiled=True),
            lax.all_gather(offsets[layer_index], "shard", axis=1, tiled=True),
        )
        (
            qkv_weight,
            qkv_bias,
            out_weight,
            up_weight,
            up_bias,
            down_weight,
            gain_rows,
            offset_rows,
        ) = current
        gain_float = gain_rows.astype(jnp.float32)
        upstream_half = upstream.astype(jnp.bfloat16)
        contraction_part = jnp.einsum(
            "rtf,rtd->fd", activation, upstream_half, preferred_element_type=jnp.float32
        )
        offset_down = jnp.sum(upstream, axis=(0, 1))
        hidden_back = jnp.einsum(
            "rtd,fd->rtf", upstream_half, down_weight, preferred_element_type=jnp.float32
        ) * gelu_slope(preact)
        hidden_half = hidden_back.astype(jnp.bfloat16)
        hidden_part = jnp.sum(hidden_back, axis=(0, 1)).reshape(up_bias.shape)
        expansion_part = jnp.einsum(
            "rtd,rtf->df", feed_input, hidden_half, preferred_element_type=jnp.float32
        )
        feed_partial = jnp.einsum(
            "rtf,df->rtd", hidden_half, up_weight, preferred_element_type=jnp.float32
        )
        feed_back = lax.psum(feed_partial.astype(jnp.bfloat16), "tensor").astype(jnp.float32)
        gain_two = jnp.sum(feed_back * normed_two, axis=(0, 1))
        offset_two = jnp.sum(feed_back, axis=(0, 1))
        middle_back = upstream + norm_backward(feed_back, normed_two, spread_two, gain_float[1])
        middle_half = middle_back.astype(jnp.bfloat16)
        mixing_part = jnp.einsum(
            "rtc,rtd->cd", attended, middle_half, preferred_element_type=jnp.float32
        )
        offset_mix = jnp.sum(middle_back, axis=(0, 1))
        attended_back = jnp.einsum(
            "rtd,cd->rtc", middle_half, out_weight, preferred_element_type=jnp.float32
        ).astype(jnp.bfloat16)
        back_heads = attended_back.reshape(row_count, block_length, heads_here, HEAD)
        attended_heads = attended.reshape(row_count, block_length, heads_here, HEAD)
        row_delta = jnp.sum(
            back_heads.astype(jnp.float32) * attended_heads.astype(jnp.float32), axis=-1
        )
        masked = masked_scores(query_block, key_block, visible, head_scale)
        soft = jnp.exp(masked - log_total)
        soft_half = soft.astype(jnp.bfloat16)
        prob_back = jnp.einsum(
            "rqhe,rkhe->rhqk", back_heads, value_block, preferred_element_type=jnp.float32
        )
        score_back = (
            soft * (prob_back - jnp.transpose(row_delta, (0, 2, 1))[..., None]) * head_scale
        ).astype(jnp.bfloat16)
        query_back = jnp.einsum(
            "rhqk,rkhe->rqhe", score_back, key_block, preferred_element_type=jnp.float32
        ).reshape(row_count, block_length, -1)
        key_full = jnp.einsum(
            "rhqk,rqhe->rkhe", score_back, query_block, preferred_element_type=jnp.float32
        ).reshape(row_count, block_length * context_size, -1)
        value_full = jnp.einsum(
            "rhqk,rqhe->rkhe", soft_half, back_heads, preferred_element_type=jnp.float32
        ).reshape(row_count, block_length * context_size, -1)
        key_back, value_back = (
            lax.psum_scatter(
                key_full.astype(jnp.bfloat16), "context", scatter_dimension=1, tiled=True
            ).astype(jnp.float32),
            lax.psum_scatter(
                value_full.astype(jnp.bfloat16), "context", scatter_dimension=1, tiled=True
            ).astype(jnp.float32),
        )
        head_part = jnp.stack(
            [jnp.sum(query_back, axis=(0, 1)), jnp.sum(value_back, axis=(0, 1))]
        ).reshape(qkv_bias.shape)
        project_back = jnp.stack([query_back, key_back, value_back]).astype(jnp.bfloat16)
        projection_part = jnp.einsum(
            "rtd,jrtc->jdc", attend_input, project_back, preferred_element_type=jnp.float32
        )
        input_partial = jnp.einsum(
            "jrtc,jdc->rtd", project_back, qkv_weight, preferred_element_type=jnp.float32
        )
        input_back = lax.psum(input_partial.astype(jnp.bfloat16), "tensor").astype(jnp.float32)
        gain_one = jnp.sum(input_back * normed_one, axis=(0, 1))
        offset_one = jnp.sum(input_back, axis=(0, 1))
        upstream = middle_back + norm_backward(input_back, normed_one, spread_one, gain_float[0])
        grad_parts = (
            projection_part,
            head_part,
            mixing_part,
            expansion_part,
            hidden_part,
            contraction_part,
            jnp.stack([gain_one, gain_two]),
            jnp.stack([offset_one, offset_two, offset_mix, offset_down]),
        )
        collected.insert(
            0,
            (
                lax.psum(
                    lax.psum_scatter(
                        grad_parts[0].astype(jnp.bfloat16), "shard", scatter_dimension=1, tiled=True
                    ),
                    "context",
                ).astype(jnp.float32),
                lax.psum(
                    lax.psum_scatter(
                        grad_parts[1].astype(jnp.bfloat16), "shard", scatter_dimension=2, tiled=True
                    ),
                    "context",
                ).astype(jnp.float32),
                lax.psum(
                    lax.psum_scatter(
                        grad_parts[2].astype(jnp.bfloat16), "shard", scatter_dimension=1, tiled=True
                    ),
                    "context",
                ).astype(jnp.float32),
                lax.psum(
                    lax.psum_scatter(
                        grad_parts[3].astype(jnp.bfloat16), "shard", scatter_dimension=0, tiled=True
                    ),
                    "context",
                ).astype(jnp.float32),
                lax.psum(
                    lax.psum_scatter(
                        grad_parts[4].astype(jnp.bfloat16), "shard", scatter_dimension=1, tiled=True
                    ),
                    "context",
                ).astype(jnp.float32),
                lax.psum(
                    lax.psum_scatter(
                        grad_parts[5].astype(jnp.bfloat16), "shard", scatter_dimension=1, tiled=True
                    ),
                    "context",
                ).astype(jnp.float32),
                lax.psum(
                    lax.psum_scatter(
                        grad_parts[6].astype(jnp.bfloat16), "shard", scatter_dimension=1, tiled=True
                    ),
                    "context",
                ).astype(jnp.float32),
                lax.psum(
                    lax.psum_scatter(
                        grad_parts[7].astype(jnp.bfloat16), "shard", scatter_dimension=1, tiled=True
                    ),
                    "context",
                ).astype(jnp.float32),
            ),
        )
    stacked = [jnp.stack([entry[member] for entry in collected]) for member in range(8)]
    return (
        stream,
        upstream,
        stacked[0],
        stacked[1],
        stacked[2],
        stacked[3],
        stacked[4],
        stacked[5],
        stacked[6],
        stacked[7],
    )


def solution(mesh):
    in_specs = (
        P("shard", "context", None),
        P("shard", "context"),
        P(None, None, "shard", "tensor"),
        P(None, None, "tensor", "shard"),
        P(None, "tensor", "shard"),
        P(None, "shard", "tensor"),
        P(None, "tensor", "shard"),
        P(None, "tensor", "shard"),
        P(None, None, "shard"),
        P(None, None, "shard"),
        P("shard", "context", None),
    )
    out_specs = (
        P("shard", "context", None),
        P("shard", "context", None),
        P(None, None, "shard", "tensor"),
        P(None, None, "tensor", "shard"),
        P(None, "tensor", "shard"),
        P(None, "shard", "tensor"),
        P(None, "tensor", "shard"),
        P(None, "tensor", "shard"),
        P(None, None, "shard"),
        P(None, None, "shard"),
    )
    return jax.shard_map(
        per_device, mesh=mesh, in_specs=in_specs, out_specs=out_specs, check_vma=False
    )
```

profile of v0, /device:TPU:0, one launch (start us, length us, event | category | flops | bytes accessed | tf_op | source)
XLA Modules:
  0.0 1538.4 jit_solution(7133893320823804238)
XLA Ops:
  10.4 25.5 %all-gather.1 = bf16[1,4,768]{1,0,2:T(2,128)(2,1)S(1)} all-gather(bf16[1,4,48]{1,0,2:T(2,128)(2,1)S(1)} %copy.288), channel_id=3, replica_groups=mesh['shard'=16,'context'=4,'tensor'=2] {'shard'}, dimensions={2}, use_global_device_ids=true | all-gather | bytes 6528 | tf_op jit(solution)/shard_map/all_gather | solution.py:81
  37.0 23.4 %all-gather = bf16[1,2,768]{1,0,2:T(2,128)(2,1)S(1)} all-gather(bf16[1,2,48]{1,0,2:T(2,128)(2,1)S(1)} %copy.287), channel_id=2, replica_groups=mesh['shard'=16,'context'=4,'tensor'=2] {'shard'}, dimensions={2}, use_global_device_ids=true | all-gather | bytes 3264 | tf_op jit(solution)/shard_map/all_gather | solution.py:80
  61.4 21.3 %all-gather.3 = bf16[1,2,6,64]{2,1,0,3:T(2,128)(2,1)S(1)} all-gather(bf16[1,2,6,4]{2,1,0,3:T(2,128)(2,1)S(1)} %copy.289), channel_id=5, replica_groups=mesh['shard'=16,'context'=4,'tensor'=2] {'shard'}, dimensions={3}, use_global_device_ids=true | all-gather | bytes 1632 | tf_op jit(solution)/shard_map/all_gather | solution.py:75
  83.1 10.0 all_gather.79
  93.1 23.6 %all-gather.5 = bf16[1,384,768]{1,2,0:T(8,128)(2,1)S(1)} all-gather(bf16[1,384,48]{1,2,0:T(8,128)(2,1)S(1)} %get-tuple-element.105), channel_id=7, replica_groups=mesh['shard'=16,'context'=4,'tensor'=2] {'shard'}, dimensions={2}, use_global_device_ids=true | all-gather | bytes 626688 | tf_op jit(solution)/shard_map/all_gather | solution.py:76
  116.9 4.6 slice_reduce_fusion.8
  121.8 11.1 slice_reduce_fusion.6
  136.1 14.4 all-gather.4
  157.7 13.3 all_gather.78
  178.1 21.1 %all-gather.7 = bf16[1,24,64]{1,0,2:T(2,128)(2,1)S(1)} all-gather(bf16[1,24,4]{1,0,2:T(2,128)(2,1)S(1)} %copy.290), channel_id=9, replica_groups=mesh['shard'=16,'context'=4,'tensor'=2] {'shard'}, dimensions={2}, use_global_device_ids=true | all-gather | bytes 3264 | tf_op jit(solution)/shard_map/all_gather | solution.py:78
  201.0 47.1 %all-gather.27.cloned.1.call-done = bf16[1,768,1536]{2,1,0:T(8,128)(2,1)} async-done(((bf16[1,48,1536]{2,1,0:T(8,128)(2,1)}), bf16[1,768,1536]{2,1,0:T(8,128)(2,1)}) %all-gather.27.cloned.1.call-update) | async-done | bytes 2359312 | tf_op jit(solution)/shard_map/all_gather | solution.py:77
  250.6 45.3 %all-gather.29.cloned.1.call-done = bf16[1,1536,768]{1,2,0:T(8,128)(2,1)} async-done(((bf16[1,1536,48]{1,2,0:T(8,128)(2,1)}), bf16[1,1536,768]{1,2,0:T(8,128)(2,1)}) %all-gather.29.cloned.1.call-update) | async-done | bytes 2359312 | tf_op jit(solution)/shard_map/all_gather | solution.py:79
  300.4 23.3 %all-gather.10 = bf16[1,4,768]{1,0,2:T(2,128)(2,1)S(1)} all-gather(bf16[1,4,48]{1,0,2:T(2,128)(2,1)S(1)} %copy.292), channel_id=12, replica_groups=mesh['shard'=16,'context'=4,'tensor'=2] {'shard'}, dimensions={2}, use_global_device_ids=true | all-gather | bytes 6528 | tf_op jit(solution)/shard_map/all_gather | solution.py:81
  324.1 22.4 %all-gather.9 = bf16[1,2,768]{1,0,2:T(2,128)(2,1)S(1)} all-gather(bf16[1,2,48]{1,0,2:T(2,128)(2,1)S(1)} %copy.291), channel_id=11, replica_groups=mesh['shard'=16,'context'=4,'tensor'=2] {'shard'}, dimensions={2}, use_global_device_ids=true | all-gather | bytes 3264 | tf_op jit(solution)/shard_map/all_gather | solution.py:80
  347.0 22.1 %all-gather.12 = bf16[1,2,6,64]{2,1,0,3:T(2,128)(2,1)S(1)} all-gather(bf16[1,2,6,4]{2,1,0,3:T(2,128)(2,1)S(1)} %copy.293), channel_id=14, replica_groups=mesh['shard'=16,'context'=4,'tensor'=2] {'shard'}, dimensions={3}, use_global_device_ids=true | all-gather | bytes 1632 | tf_op jit(solution)/shard_map/all_gather | solution.py:75
  370.5 24.7 %all-gather.14 = bf16[1,384,768]{1,2,0:T(8,128)(2,1)} all-gather(bf16[1,384,48]{1,2,0:T(8,128)(2,1)S(1)} %get-tuple-element.104), channel_id=16, replica_groups=mesh['shard'=16,'context'=4,'tensor'=2] {'shard'}, dimensions={2}, use_global_device_ids=true | all-gather | bytes 626688 | tf_op jit(solution)/shard_map/all_gather | solution.py:76
  395.3 4.6 slice_reduce_fusion.2
  399.9 10.9 slice_reduce_fusion
  415.9 15.0 all-gather.13
  437.9 14.1 all_gather.89
  460.3 22.7 %all-gather.16 = bf16[1,24,64]{1,0,2:T(2,128)(2,1)S(1)} all-gather(bf16[1,24,4]{1,0,2:T(2,128)(2,1)S(1)} %copy.294), channel_id=18, replica_groups=mesh['shard'=16,'context'=4,'tensor'=2] {'shard'}, dimensions={2}, use_global_device_ids=true | all-gather | bytes 3264 | tf_op jit(solution)/shard_map/all_gather | solution.py:78
  486.4 45.0 %all-gather.33.cloned.1.call-done = bf16[1,768,1536]{2,1,0:T(8,128)(2,1)} async-done(((bf16[1,48,1536]{2,1,0:T(8,128)(2,1)}), bf16[1,768,1536]{2,1,0:T(8,128)(2,1)}) %all-gather.33.cloned.1.call-update) | async-done | bytes 2359312 | tf_op jit(solution)/shard_map/all_gather | solution.py:77
  531.4 3.7 convolution_add_fusion
  535.1 43.8 %all-gather.35.cloned.1.call-done = bf16[1,1536,768]{1,2,0:T(8,128)(2,1)} async-done(((bf16[1,1536,48]{1,2,0:T(8,128)(2,1)}), bf16[1,1536,768]{1,2,0:T(8,128)(2,1)}) %all-gather.35.cloned.1.call-update) | async-done | bytes 2359312 | tf_op jit(solution)/shard_map/all_gather | solution.py:79
  578.8 4.5 fusion.157
  585.8 4.1 fusion.3
  590.2 19.0 %all-reduce.36.cloned.1.call-done = bf16[2,128,768]{2,1,0:T(8,128)(2,1)} async-done(((bf16[2,128,768]{2,1,0:T(8,128)(2,1)}), bf16[2,128,768]{2,1,0:T(8,128)(2,1)}) %all-reduce.36.cloned.1.call-update) | async-done | bytes 393232 | tf_op jit(solution)/shard_map/psum | solution.py:218
  611.7 26.7 %all-reduce.34.cloned.1.call-done = f32[2,128,768]{2,1,0:T(8,128)} async-done(((f32[2,128,768]{2,1,0:T(8,128)}), f32[2,128,768]{2,1,0:T(8,128)}) %all-reduce.34.cloned.1.call-update) | async-done | bytes 786448 | tf_op jit(solution)/shard_map/psum | solution.py:140
  655.0 3.8 convolution_convert_fusion.2
  664.4 14.6 reduce-scatter.21.cloned.1.call-done
  678.9 24.7 %reduce-scatter.23.cloned.1.call-done = bf16[2,128,384]{2,1,0:T(8,128)(2,1)} async-done(((bf16[2,512,384]{2,1,0:T(8,128)(2,1)}), bf16[2,128,384]{2,1,0:T(8,128)(2,1)}) %reduce-scatter.23.cloned.1.call-update) | async-done | bytes 196624 | tf_op jit(solution)/shard_map/reduce_scatter | solution.py:257
  707.0 24.0 %all-reduce.38.cloned.1.call-done = bf16[2,128,768]{2,1,0:T(8,128)(2,1)} async-done(((bf16[2,128,768]{2,1,0:T(8,128)(2,1)}), bf16[2,128,768]{2,1,0:T(8,128)(2,1)}) %all-reduce.38.cloned.1.call-update) | async-done | bytes 393232 | tf_op jit(solution)/shard_map/psum | solution.py:271
  738.6 25.5 %all-reduce.40.cloned.1.call-done = bf16[2,128,768]{2,1,0:T(8,128)(2,1)} async-done(((bf16[2,128,768]{2,1,0:T(8,128)(2,1)}), bf16[2,128,768]{2,1,0:T(8,128)(2,1)}) %all-reduce.40.cloned.1.call-update) | async-done | bytes 393232 | tf_op jit(solution)/shard_map/psum | solution.py:218
  780.5 3.9 convolution_convert_fusion
  791.5 12.6 reduce-scatter.25.cloned.1.call-done
  804.2 24.6 %reduce-scatter.27.cloned.1.call-done = bf16[2,128,384]{2,1,0:T(8,128)(2,1)} async-done(((bf16[2,512,384]{2,1,0:T(8,128)(2,1)}), bf16[2,128,384]{2,1,0:T(8,128)(2,1)}) %reduce-scatter.27.cloned.1.call-update) | async-done | bytes 196624 | tf_op jit(solution)/shard_map/reduce_scatter | solution.py:257
  840.2 5.3 copy.244
  847.6 5.2 copy.242
  857.4 3.9 bitcast_convert_fusion
  875.2 75.6 %all-reduce.12 = (bf16[2,6,64]{1,0,2:T(2,128)(2,1)S(1)}, bf16[2,6,64]{1,0,2:T(2,128)(2,1)S(1)}, bf16[24,64]{1,0:T(8,128)(2,1)S(1)}, bf16[24,64]{1,0:T(8,128)(2,1...) all-reduce(bf16[2,6,64]{1,0,2:T(2,128)(2,1)S(1)} %copy.249, ...), channel_id=27, replica_groups=mesh['shard'=16,'context'=4,'tensor'=2] {'shard'}, use_global_device_ids=true, to_apply=%region_44.45.clone | all-reduce | flops 13824 | bytes 55296
  955.9 52.0 %reduce-scatter.37.cloned.1.call-done = bf16[384,48]{0,1:T(8,128)(2,1)} async-done(((bf16[384,768]{0,1:T(8,128)(2,1)}), bf16[384,48]{0,1:T(8,128)(2,1)}) %reduce-scatter.37.cloned.1.call-update) | async-done | bytes 36880
  1008.0 111.1 %all-reduce.44.cloned.1.call-done = (bf16[3,768,384]{2,0,1:T(4,128)(2,1)}, bf16[3,768,384]{2,0,1:T(4,128)(2,1)}) async-done(((bf16[3,768,384]{2,0,1:T(4,128)(2,1)}, bf16[3,768,384]{2,0,1:T(4,128)(2,1)}), (bf16[3,768,384]{2,0,1:T(4,128)(2,1)}, bf16[3,768,384]{2,0,1:T(4,128)(2,1)})) %all-reduce.44.cloned.1.call-update) | async-done | bytes 3538960
  1122.4 75.1 %reduce-scatter.31.cloned.1.call-done = bf16[48,1536]{1,0:T(8,128)(2,1)} async-done(((bf16[768,1536]{1,0:T(8,128)(2,1)}), bf16[48,1536]{1,0:T(8,128)(2,1)}) %reduce-scatter.31.cloned.1.call-update) | async-done | bytes 147472 | tf_op jit(solution)/shard_map/reduce_scatter | solution.py:307
  1197.5 77.9 %reduce-scatter.35.cloned.1.call-done = bf16[1536,48]{0,1:T(8,128)(2,1)} async-done(((bf16[1536,768]{0,1:T(8,128)(2,1)}), bf16[1536,48]{0,1:T(8,128)(2,1)}) %reduce-scatter.35.cloned.1.call-update) | async-done | bytes 147472 | tf_op jit(solution)/shard_map/reduce_scatter | solution.py:319
  1275.3 77.7 %reduce-scatter.29.cloned.1.call-done = bf16[48,1536]{1,0:T(8,128)(2,1)} async-done(((bf16[768,1536]{1,0:T(8,128)(2,1)}), bf16[48,1536]{1,0:T(8,128)(2,1)}) %reduce-scatter.29.cloned.1.call-update) | async-done | bytes 147472 | tf_op jit(solution)/shard_map/reduce_scatter | solution.py:307
  1353.0 77.9 %reduce-scatter.33.cloned.1.call-done = bf16[1536,48]{0,1:T(8,128)(2,1)} async-done(((bf16[1536,768]{0,1:T(8,128)(2,1)}), bf16[1536,48]{0,1:T(8,128)(2,1)}) %reduce-scatter.33.cloned.1.call-update) | async-done | bytes 147472 | tf_op jit(solution)/shard_map/reduce_scatter | solution.py:319
  1432.2 43.3 %all-reduce.46.cloned.1.call-done = (bf16[1,2,6,4]{2,3,1,0:T(4,128)(2,1)}, bf16[1,2,6,4]{2,3,1,0:T(4,128)(2,1)}, bf16[1,384,48]{1,2,0:T(8,128)(2,1)}, bf16[1,384...) async-done(((bf16[1,2,6,4]{2,3,1,0:T(4,128)(2,1)}, ...) | async-done | bytes 75472 | tf_op jit(solution)/shard_map/psum | solution.py:294
  1482.0 42.9 %all-reduce.48.cloned.1.call-done = (bf16[1,3,48,384]{3,1,2,0:T(4,128)(2,1)}, bf16[1,3,48,384]{3,1,2,0:T(4,128)(2,1)}, bf16[1,48,1536]{2,1,0:T(8,128)(2,1)}, bf1...) async-done(((bf16[1,3,48,384]{3,1,2,0:T(4,128)(2,1)}, bf16[1,3,48,384]{3,1,2,0:T(4,128)(2,1)}, bf16[1,48,1536]{2,1,0:T(8,128)(2,1)}, ...) | async-done | bytes 811024 | tf_op jit(solution)/shard_map/psum | solution.py:288
  (425 shorter events, 172.4 us)
Async XLA Ops:
  7.2 29.1 %copy-start.83 = (bf16[2,2,48]{2,1,0:T(2,128)(2,1)S(1)}, bf16[2,2,48]{2,1,0:T(2,128)(2,1)}, u32[]{:S(2)}) copy-start(bf16[2,2,48]{2,1,0:T(2,128)(2,1)} %param.19) | copy-start | bytes 1156
  7.2 53.6 %copy-start.88 = (s32[2,128]{1,0:T(2,128)S(1)}, s32[2,128]{1,0:T(2,128)}, u32[]{:S(2)}) copy-start(s32[2,128]{1,0:T(2,128)} %param.12) | copy-start | bytes 3076
  7.2 53.6 %copy-start.76 = (bf16[2,2,6,4]{2,3,1,0:T(4,128)(2,1)S(1)}, bf16[2,2,6,4]{2,3,1,0:T(4,128)(2,1)}, u32[]{:S(2)}) copy-start(bf16[2,2,6,4]{2,3,1,0:T(4,128)(2,1)} %param.14) | copy-start | bytes 580
  7.2 75.7 %copy-start = (f32[2,128,768]{2,1,0:T(8,128)S(1)}, f32[2,128,768]{2,1,0:T(8,128)}, u32[]{:S(2)}) copy-start(f32[2,128,768]{2,1,0:T(8,128)} %param.11) | copy-start | bytes 2359300
  7.2 125.7 %all-gather.25.cloned.1.call-start = ((), (), s32[]{:S(2)}) async-start(), calls=%async_computation.26 | async-start | bytes 1880064 | tf_op jit(solution)/shard_map/all_gather | solution.py:74
  9.0 84.1 %copy-start.41 = (bf16[2,384,48]{1,2,0:T(8,128)(2,1)S(1)}, bf16[2,384,48]{1,2,0:T(8,128)(2,1)}, u32[]{:S(2)}) copy-start(bf16[2,384,48]{1,2,0:T(8,128)(2,1)} %param.15) | copy-start | bytes 221188
  9.0 190.4 %all-reduce.28.cloned.1.call-start = ((), (), s32[]{:S(2)}) async-start(), calls=%async_computation.10 | async-start | bytes 1572864 | tf_op jit(solution)/shard_map/psum | solution.py:130
  82.8 71.3 %copy-start.50 = (f32[6,64]{1,0:T(8,128)}, f32[6,64]{1,0:T(8,128)S(1)}, u32[]{:S(2)}) copy-start(f32[6,64]{1,0:T(8,128)S(1)} %copy.213) | copy-start | bytes 4612
  116.7 57.8 %copy-start.10 = (bf16[1,384,768]{1,2,0:T(8,128)(2,1)}, bf16[1,384,768]{1,2,0:T(8,128)(2,1)S(1)}, u32[]{:S(2)}) copy-start(bf16[1,384,768]{1,2,0:T(8,128)(2,1)S(1)} %all-gather.5) | copy-start | bytes 1769476
  121.8 49.5 %copy-start.20 = (pred[2,128,512]{2,1,0:T(8,128)(4,1)}, pred[2,128,512]{2,1,0:T(8,128)(4,1)S(1)}, u32[]{:S(2)}) copy-start(pred[2,128,512]{2,1,0:T(8,128)(4,1)S(1)} %compare_and_fusion) | copy-start | bytes 393220
  132.9 115.1 %copy-start.61 = (f32[768]{0:T(1024)}, f32[768]{0:T(1024)S(1)}, u32[]{:S(2)}) copy-start(f32[768]{0:T(1024)S(1)} %get-tuple-element.49) | copy-start | bytes 9220
  175.8 72.3 %all-gather.27.cloned.1.call-start = ((), (), s32[]{:S(2)}) async-start(), calls=%async_computation.27 | async-start | bytes 2506752 | tf_op jit(solution)/shard_map/all_gather | solution.py:77
  176.6 119.3 %all-gather.29.cloned.1.call-start = ((), (), s32[]{:S(2)}) async-start(), calls=%async_computation.28 | async-start | bytes 2506752 | tf_op jit(solution)/shard_map/all_gather | solution.py:79
  177.4 233.4 %all-reduce.30.cloned.1.call-start = ((), (), s32[]{:S(2)}) async-start(), calls=%async_computation.11 | async-start | bytes 1572864 | tf_op jit(solution)/shard_map/psum | solution.py:140
  200.7 49.9 %copy-start.55 = (f32[2,128]{1,0:T(2,128)}, f32[2,128]{1,0:T(2,128)S(1)}, u32[]{:S(2)}) copy-start(f32[2,128]{1,0:T(2,128)S(1)} %broadcast_multiply_fusion.10) | copy-start | bytes 3076
  200.9 49.7 %copy-start.64 = (f32[2,128]{1,0:T(2,128)}, f32[2,128]{1,0:T(2,128)S(1)}, u32[]{:S(2)}) copy-start(f32[2,128]{1,0:T(2,128)S(1)} %add_rsqrt_fusion.2) | copy-start | bytes 3076
  250.6 45.3 %copy-start.90 = (f32[2,128,1536]{2,1,0:T(8,128)}, f32[2,128,1536]{2,1,0:T(8,128)S(1)}, u32[]{:S(2)}) copy-start(f32[2,128,1536]{2,1,0:T(8,128)S(1)} %convolution_add_fusion.1) | copy-start | bytes 4718596
  250.6 49.6 %copy-start.79 = (bf16[1,4,48]{2,1,0:T(4,128)(2,1)S(1)}, bf16[1,4,48]{2,1,0:T(4,128)(2,1)}, u32[]{:S(2)}) copy-start(bf16[1,4,48]{2,1,0:T(4,128)(2,1)} %get-tuple-element.115) | copy-start | bytes 1156
  299.6 47.4 %copy-start.75 = (bf16[1,2,6,4]{2,3,1,0:T(4,128)(2,1)S(1)}, bf16[1,2,6,4]{2,3,1,0:T(4,128)(2,1)}, u32[]{:S(2)}) copy-start(bf16[1,2,6,4]{2,3,1,0:T(4,128)(2,1)} %get-tuple-element.110) | copy-start | bytes 292
  299.6 112.8 %all-gather.31.cloned.1.call-start = ((), (), s32[]{:S(2)}) async-start(), calls=%async_computation.29 | async-start | bytes 1880064 | tf_op jit(solution)/shard_map/all_gather | solution.py:74
  300.2 183.5 %all-reduce.32.cloned.1.call-start = ((), (), s32[]{:S(2)}) async-start(), calls=%async_computation.12 | async-start | bytes 1572864 | tf_op jit(solution)/shard_map/psum | solution.py:130
  457.4 26.4 %copy-start.28 = (bf16[2,6,64,128]{3,2,1,0:T(8,128)(2,1)}, bf16[2,6,64,128]{3,2,1,0:T(8,128)(2,1)S(1)}, u32[]{:S(2)}) copy-start(bf16[2,6,64,128]{3,2,1,0:T(8,128)(2,1)S(1)} %convolution_convert_fusion.4) | copy-start | bytes 589828
  458.7 72.7 %all-gather.33.cloned.1.call-start = ((), (), s32[]{:S(2)}) async-start(), calls=%async_computation.30 | async-start | bytes 2506752 | tf_op jit(solution)/shard_map/all_gather | solution.py:77
  459.5 119.4 %all-gather.35.cloned.1.call-start = ((), (), s32[]{:S(2)}) async-start(), calls=%async_computation.31 | async-start | bytes 2506752 | tf_op jit(solution)/shard_map/all_gather | solution.py:79
  460.2 149.0 %all-reduce.36.cloned.1.call-start = ((), (), s32[]{:S(2)}) async-start(), calls=%async_computation.14 | async-start | bytes 786432 | tf_op jit(solution)/shard_map/psum | solution.py:218
  585.7 52.6 %all-reduce.34.cloned.1.call-start = ((), (), s32[]{:S(2)}) async-start(), calls=%async_computation.13 | async-start | bytes 1572864 | tf_op jit(solution)/shard_map/psum | solution.py:140
  589.9 89.0 %reduce-scatter.21.cloned.1.call-start = ((), (), s32[]{:S(2)}) async-start(), calls=%async_computation.15 | async-start | bytes 983040 | tf_op jit(solution)/shard_map/reduce_scatter | solution.py:254
  654.9 48.7 %reduce-scatter.23.cloned.1.call-start = ((), (), s32[]{:S(2)}) async-start(), calls=%async_computation.16 | async-start | bytes 983040 | tf_op jit(solution)/shard_map/reduce_scatter | solution.py:257
  661.1 69.9 %all-reduce.38.cloned.1.call-start = ((), (), s32[]{:S(2)}) async-start(), calls=%async_computation.17 | async-start | bytes 786432 | tf_op jit(solution)/shard_map/psum | solution.py:271
  703.7 27.3 %copy-start.49 = (f32[2,128]{1,0:T(2,128)S(1)}, f32[2,128]{1,0:T(2,128)}, u32[]{:S(2)}) copy-start(f32[2,128]{1,0:T(2,128)} %copy-done.48) | copy-start | bytes 3076
  703.7 27.3 %copy-start.58 = (f32[2,128]{1,0:T(2,128)S(1)}, f32[2,128]{1,0:T(2,128)}, u32[]{:S(2)}) copy-start(f32[2,128]{1,0:T(2,128)} %copy-done.57) | copy-start | bytes 3076
  706.9 57.2 %all-reduce.40.cloned.1.call-start = ((), (), s32[]{:S(2)}) async-start(), calls=%async_computation.18 | async-start | bytes 786432 | tf_op jit(solution)/shard_map/psum | solution.py:218
  737.0 27.1 %copy-start.56 = (f32[2,128]{1,0:T(2,128)S(1)}, f32[2,128]{1,0:T(2,128)}, u32[]{:S(2)}) copy-start(f32[2,128]{1,0:T(2,128)} %copy-done.55) | copy-start | bytes 3076
  737.0 27.1 %copy-start.65 = (f32[2,128]{1,0:T(2,128)S(1)}, f32[2,128]{1,0:T(2,128)}, u32[]{:S(2)}) copy-start(f32[2,128]{1,0:T(2,128)} %copy-done.64) | copy-start | bytes 3076
  738.6 65.6 %reduce-scatter.25.cloned.1.call-start = ((), (), s32[]{:S(2)}) async-start(), calls=%async_computation.19 | async-start | bytes 983040 | tf_op jit(solution)/shard_map/reduce_scatter | solution.py:254
  780.2 48.5 %reduce-scatter.27.cloned.1.call-start = ((), (), s32[]{:S(2)}) async-start(), calls=%async_computation.20 | async-start | bytes 983040 | tf_op jit(solution)/shard_map/reduce_scatter | solution.py:257
  786.7 85.9 %all-reduce.42.cloned.1.call-start = ((), (), s32[]{:S(2)}) async-start(), calls=%async_computation.21 | async-start | bytes 786432 | tf_op jit(solution)/shard_map/psum | solution.py:271
  832.0 123.9 %reduce-scatter.39.cloned.1.call-start = ((), (), s32[]{:S(2)}) async-start(), calls=%async_computation.33 | async-start | bytes 626688
  834.6 173.4 %reduce-scatter.37.cloned.1.call-start = ((), (), s32[]{:S(2)}) async-start(), calls=%async_computation.32 | async-start | bytes 626688
  837.0 282.1 %all-reduce.44.cloned.1.call-start = ((), (), s32[]{:S(2)}) async-start(), calls=%async_computation.34 | async-start | bytes 9437184
  852.8 344.7 %reduce-scatter.31.cloned.1.call-start = ((), (), s32[]{:S(2)}) async-start(), calls=%async_computation.23 | async-start | bytes 2506752 | tf_op jit(solution)/shard_map/reduce_scatter | solution.py:307
  856.3 419.0 %reduce-scatter.35.cloned.1.call-start = ((), (), s32[]{:S(2)}) async-start(), calls=%async_computation.25 | async-start | bytes 2506752 | tf_op jit(solution)/shard_map/reduce_scatter | solution.py:319
  861.3 491.7 %reduce-scatter.29.cloned.1.call-start = ((), (), s32[]{:S(2)}) async-start(), calls=%async_computation.22 | async-start | bytes 2506752 | tf_op jit(solution)/shard_map/reduce_scatter | solution.py:307
  864.8 566.1 %reduce-scatter.33.cloned.1.call-start = ((), (), s32[]{:S(2)}) async-start(), calls=%async_computation.24 | async-start | bytes 2506752 | tf_op jit(solution)/shard_map/reduce_scatter | solution.py:319
  868.9 606.6 %all-reduce.46.cloned.1.call-start = ((), (), s32[]{:S(2)}) async-start(), calls=%async_computation.35 | async-start | bytes 165888 | tf_op jit(solution)/shard_map/psum | solution.py:294
  872.4 558.6 %copy-start.4 = (f32[2,128,768]{2,1,0:T(8,128)S(1)}, f32[2,128,768]{2,1,0:T(8,128)}, u32[]{:S(2)}) copy-start(f32[2,128,768]{2,1,0:T(8,128)} %copy-done.3) | copy-start | bytes 2359300
  872.6 558.4 %copy-start.19 = (bf16[2,128,768]{2,1,0:T(8,128)(2,1)S(1)}, bf16[2,128,768]{2,1,0:T(8,128)(2,1)}, u32[]{:S(2)}) copy-start(bf16[2,128,768]{2,1,0:T(8,128)(2,1)} %all-reduce.42.cloned.1.call-done) | copy-start | bytes 1179652
  1008.0 516.9 %all-reduce.48.cloned.1.call-start = ((), (), s32[]{:S(2)}) async-start(), calls=%async_computation.36 | async-start | bytes 1769472 | tf_op jit(solution)/shard_map/psum | solution.py:288
  (72 other events, 288.1 us)
Sparse Core Ops, SparseCore 0:
  10.8 47.1 all-gather.24
  175.9 21.9 all-reduce.27
  200.9 47.1 all-gather.26
  250.9 45.0 all-gather.28
  299.7 24.0 all-reduce.29
  325.8 46.3 all-gather.30
  458.8 22.3 all-reduce.31
  484.2 47.1 all-gather.32
  533.7 45.0 all-gather.34
  585.9 23.2 all-reduce.35
  612.2 26.1 all-reduce.33
  655.0 23.8 reduce-scatter.20
  681.4 22.1 reduce-scatter.22
  707.1 23.8 all-reduce.37
  738.7 25.3 all-reduce.39
  780.3 23.7 reduce-scatter.24
  806.5 22.1 reduce-scatter.26
  832.1 23.8 all-reduce.41
  859.8 73.2 reduce-scatter.38
  936.8 71.1 reduce-scatter.36
  1011.4 107.6 all-reduce.43
  1122.8 74.6 reduce-scatter.30
  1201.1 74.1 reduce-scatter.34
  1278.9 74.1 reduce-scatter.28
  1356.7 74.2 reduce-scatter.32
  1435.3 40.1 all-reduce.45
  1478.7 46.2 all-reduce.47
where the time goes:
time: 1540 us
  waiting for transfers between devices  913 us (59%)
  blocking collectives  372 us (24%)
  local copies, waits for them, and re-layouts  100 us (6%)
  matrix products  92.7 us (6%)
  other arithmetic  40.6 us (3%)
  between operations  17.4 us (1%)
    unnamed x30, waiting for transfers between devices  165 us
    reduce_scatter x2, waiting for transfers between devices, per_device(): lax.psum_scatter(grad_parts[5].astype(jnp.bfloat16), 'shard', scatter_dim...  156 us
    reduce_scatter x2, waiting for transfers between devices, per_device(): lax.psum_scatter(grad_parts[3].astype(jnp.bfloat16), 'shard', scatter_dim...  153 us
    all_gather x2, waiting for transfers between devices, per_device(): lax.all_gather(expansion[layer_index], 'shard', axis=0, tiled=True)  92.1 us
    all_gather x2, waiting for transfers between devices, per_device(): lax.all_gather(contraction[layer_index], 'shard', axis=1, tiled=True)  89.1 us
    unnamed x1, blocking collectives  75.6 us
    reduce_scatter x2, waiting for transfers between devices, per_device(): lax.psum_scatter(value_full.astype(jnp.bfloat16), 'context', scatter_dime...  49.3 us
    all_gather x2, blocking collectives, per_device(): lax.all_gather(offsets[layer_index], 'shard', axis=1, tiled=True)  48.7 us
  transfers between devices with their start and end apart: 27, of which 20 were waited for; matrix products, arithmetic and copies ran while one was open for 9% of the time, Pallas kernels for 0%

commit v1 on v0

v1 whole, which is shorter than its diff:
```python
import jax
import jax.numpy as jnp
from jax import lax
from jax.sharding import PartitionSpec as P

HEAD = 64

EPS = 1e-05
GELU_COEF = 0.7978845608028654
GELU_CUBE = 0.044715
MASKED = -1e30
HALF = jnp.bfloat16
FULL = jnp.float32


def gelu_value(preact):
    inner_arg = GELU_COEF * (preact + GELU_CUBE * preact * preact * preact)
    return 0.5 * preact * (1.0 + jnp.tanh(inner_arg))


def gelu_slope(preact):
    inner_arg = GELU_COEF * (preact + GELU_CUBE * preact * preact * preact)
    tanh_value = jnp.tanh(inner_arg)
    return 0.5 * (1.0 + tanh_value) + 0.5 * preact * (1.0 - tanh_value * tanh_value) * GELU_COEF * (
        1.0 + 3.0 * GELU_CUBE * preact * preact
    )


def norm_forward(stream):
    center = stream - jnp.mean(stream, axis=-1, keepdims=True)
    spread = lax.rsqrt(jnp.mean(center * center, axis=-1, keepdims=True) + EPS)
    return (center * spread, spread)


def norm_backward(upstream, normed, spread, gain_row):
    scaled = upstream * gain_row
    first_mean = jnp.mean(scaled, axis=-1, keepdims=True)
    second_mean = jnp.mean(scaled * normed, axis=-1, keepdims=True)
    return spread * (scaled - first_mean - normed * second_mean)


def dot(left, right, left_dim, right_dim):
    return lax.dot_general(
        left, right, (((left_dim,), (right_dim,)), ((), ())), preferred_element_type=FULL
    )


def pair_sum(part):
    size = lax.axis_size("tensor")
    other = lax.ppermute(part, "tensor", [(i, (i + 1) % size) for i in range(size)])
    return part.astype(FULL) + other.astype(FULL)


def from_before(block, steps):
    size = lax.axis_size("context")
    return lax.ppermute(block, "context", [(i, i + steps) for i in range(size - steps)])


def from_after(block, steps):
    size = lax.axis_size("context")
    return lax.ppermute(block, "context", [(i + steps, i) for i in range(size - steps)])


def context_sum(part):
    size = lax.axis_size("context")
    total = part.astype(FULL)
    for steps in range(1, size):
        moved = lax.ppermute(part, "context", [(i, (i + steps) % size) for i in range(size)])
        total = total + moved.astype(FULL)
    return total


def masked_scores(query_block, key_block, visible, head_scale):
    scores = (
        jnp.einsum("rqhe,rkhe->rhqk", query_block, key_block, preferred_element_type=FULL)
        * head_scale
    )
    return jnp.where(visible, scores, MASKED)


def per_device(
    inputs,
    segment_ids,
    projection,
    head_bias,
    mixing,
    expansion,
    hidden_bias,
    contraction,
    norm_gains,
    offsets,
    cotangent,
):
    layers = projection.shape[0]
    rows, block, width = inputs.shape
    shards = lax.axis_size("shard")
    contexts = lax.axis_size("context")
    own = projection.shape[2]
    heads = head_bias.shape[2]
    head_cols = projection.shape[3]
    hidden = expansion.shape[2]
    tokens = rows * block
    head_scale = HEAD ** (-0.5)
    back_steps = 2

    gathered = []
    for layer in range(layers):
        packed = jnp.concatenate(
            [projection[layer, 0], projection[layer, 1], projection[layer, 2], mixing[layer].T,
             expansion[layer], contraction[layer].T], axis=1)
        gathered.append(lax.all_gather(packed, "shard", axis=0, tiled=True))
    small_parts = [norm_gains, offsets, head_bias, hidden_bias]
    small_sizes = [part.size for part in small_parts]
    small_total = sum(small_sizes)
    small_padded = -(-small_total // 1024) * 1024
    small = jnp.concatenate([part.reshape(-1) for part in small_parts] + [jnp.zeros((small_padded - small_total,), HALF)])
    small = jnp.broadcast_to(small.reshape(1, -1, 128), (shards, small_padded // 128, 128))
    small = lax.all_to_all(small, "shard", 0, 0).reshape(shards, small_padded)

    def widen(index):
        start = sum(small_sizes[:index])
        shape = small_parts[index].shape
        piece = small[:, start:start + small_sizes[index]].astype(FULL).reshape((shards,) + shape)
        piece = jnp.moveaxis(piece, 0, -2)
        return piece.reshape(shape[:-1] + (shards * shape[-1],))

    gains_all, offsets_all = widen(0), widen(1)
    head_all = widen(2).reshape(layers, 2, head_cols)
    hidden_all = widen(3).reshape(layers, hidden)

    seg_before = [from_before(segment_ids, steps) for steps in range(back_steps, 0, -1)]
    segments_all = jnp.concatenate(seg_before + [segment_ids], axis=1)
    query_pos = jnp.arange(block, dtype=jnp.int32) + back_steps * block
    key_pos = jnp.arange((back_steps + 1) * block, dtype=jnp.int32)
    first_key = (back_steps - lax.axis_index("context")) * block
    visible = (segments_all[:, None, :] == segment_ids[:, :, None]) & (
        key_pos[None, None, :] <= query_pos[None, :, None]
    ) & (key_pos >= first_key)[None, None, :]
    visible = visible[:, None]

    def split_weights(weights):
        ends = [3 * head_cols, 4 * head_cols, 4 * head_cols + hidden, 4 * head_cols + 2 * hidden]
        return (weights[:, :ends[0]], weights[:, ends[0]:ends[1]], weights[:, ends[1]:ends[2]], weights[:, ends[2]:ends[3]])

    stream = inputs.reshape(tokens, width)
    kept = []
    for layer in range(layers):
        qkv_weight, out_weight, up_weight, down_weight = split_weights(gathered[layer])
        gain, offset = gains_all[layer], offsets_all[layer]
        normed_one, spread_one = norm_forward(stream)
        attend_input = (normed_one * gain[0] + offset[0]).astype(HALF)
        zero_bias = jnp.zeros((head_cols,), FULL)
        bias = jnp.concatenate([head_all[layer, 0], zero_bias, head_all[layer, 1]])
        projected = (dot(attend_input, qkv_weight, 1, 0) + bias).astype(HALF)
        query_rows = projected[:, :head_cols]
        key_value = projected[:, head_cols:].reshape(rows, block, 2 * head_cols)
        before = [from_before(key_value, steps) for steps in range(back_steps, 0, -1)]
        key_value_all = jnp.concatenate(before + [key_value], axis=1)
        query_block = query_rows.reshape(rows, block, heads, HEAD)
        key_block = key_value_all[:, :, :head_cols].reshape(rows, -1, heads, HEAD)
        value_block = key_value_all[:, :, head_cols:].reshape(rows, -1, heads, HEAD)
        masked = masked_scores(query_block, key_block, visible, head_scale)
        row_top = jnp.max(masked, axis=-1, keepdims=True)
        log_total = row_top + jnp.log(jnp.sum(jnp.exp(masked - row_top), axis=-1, keepdims=True))
        soft_half = jnp.exp(masked - log_total).astype(HALF)
        attended = (
            jnp.einsum("rhqk,rkhe->rqhe", soft_half, value_block, preferred_element_type=FULL)
            .astype(HALF)
            .reshape(tokens, head_cols)
        )
        middle = stream + pair_sum(dot(attended, out_weight, 1, 1)) + offset[2]
        normed_two, spread_two = norm_forward(middle)
        feed_input = (normed_two * gain[1] + offset[1]).astype(HALF)
        preact = dot(feed_input, up_weight, 1, 0) + hidden_all[layer]
        activation = gelu_value(preact).astype(HALF)
        stream = middle + pair_sum(dot(activation, down_weight, 1, 1)) + offset[3]
        kept.append((normed_one, spread_one, attend_input, query_block, key_block, value_block,
                     log_total, attended, normed_two, spread_two, feed_input, preact, activation))

    def scatter(parts):
        packed = jnp.concatenate([part.astype(HALF) for part in parts], axis=1)
        return lax.psum_scatter(packed, "shard", scatter_dimension=0, tiled=True)

    upstream = cotangent.reshape(tokens, width)
    feed_shares, attend_shares, vectors = [None] * layers, [None] * layers, [None] * layers
    for layer in reversed(range(layers)):
        (normed_one, spread_one, attend_input, query_block, key_block, value_block,
         log_total, attended, normed_two, spread_two, feed_input, preact, activation) = kept[layer]
        qkv_weight, out_weight, up_weight, down_weight = split_weights(gathered[layer])
        gain = gains_all[layer]
        upstream_half = upstream.astype(HALF)
        contraction_part = dot(upstream_half, activation, 0, 0)
        offset_down = jnp.sum(upstream, axis=0)
        hidden_back = dot(upstream_half, down_weight, 1, 0) * gelu_slope(preact)
        hidden_half = hidden_back.astype(HALF)
        hidden_part = jnp.sum(hidden_back, axis=0)
        expansion_part = dot(feed_input, hidden_half, 0, 0)
        feed_shares[layer] = scatter([expansion_part, contraction_part])
        feed_back = pair_sum(dot(hidden_half, up_weight, 1, 1).astype(HALF))
        gain_two = jnp.sum(feed_back * normed_two, axis=0)
        offset_two = jnp.sum(feed_back, axis=0)
        middle_back = upstream + norm_backward(feed_back, normed_two, spread_two, gain[1])
        middle_half = middle_back.astype(HALF)
        mixing_part = dot(middle_half, attended, 0, 0)
        offset_mix = jnp.sum(middle_back, axis=0)
        attended_back = dot(middle_half, out_weight, 1, 0).astype(HALF)
        back_heads = attended_back.reshape(rows, block, heads, HEAD)
        attended_heads = attended.reshape(rows, block, heads, HEAD)
        row_delta = jnp.sum(back_heads.astype(FULL) * attended_heads.astype(FULL), axis=-1)
        masked = masked_scores(query_block, key_block, visible, head_scale)
        soft = jnp.exp(masked - log_total)
        soft_half = soft.astype(HALF)
        prob_back = jnp.einsum("rqhe,rkhe->rhqk", back_heads, value_block, preferred_element_type=FULL)
        score_back = (
            soft * (prob_back - jnp.transpose(row_delta, (0, 2, 1))[..., None]) * head_scale
        ).astype(HALF)
        query_back = jnp.einsum(
            "rhqk,rkhe->rqhe", score_back, key_block, preferred_element_type=FULL
        ).reshape(tokens, head_cols)
        key_full = jnp.einsum(
            "rhqk,rqhe->rkhe", score_back, query_block, preferred_element_type=FULL
        ).reshape(rows, -1, head_cols)
        value_full = jnp.einsum(
            "rhqk,rqhe->rkhe", soft_half, back_heads, preferred_element_type=FULL
        ).reshape(rows, -1, head_cols)
        both_full = jnp.concatenate([key_full, value_full], axis=2)
        both_back = both_full[:, back_steps * block:]
        for steps in range(1, back_steps + 1):
            start = (back_steps - steps) * block
            both_back = both_back + from_after(both_full[:, start:start + block].astype(HALF), steps).astype(FULL)
        both_back = both_back.reshape(tokens, 2 * head_cols)
        head_part = jnp.concatenate([jnp.sum(query_back, axis=0), jnp.sum(both_back[:, head_cols:], axis=0)])
        project_back = jnp.concatenate([query_back, both_back], axis=1).astype(HALF)
        projection_part = dot(attend_input, project_back, 0, 0)
        attend_shares[layer] = scatter([projection_part, mixing_part])
        input_back = pair_sum(dot(project_back, qkv_weight, 1, 1).astype(HALF))
        gain_one = jnp.sum(input_back * normed_one, axis=0)
        offset_one = jnp.sum(input_back, axis=0)
        upstream = middle_back + norm_backward(input_back, normed_one, spread_one, gain[0])
        vectors[layer] = ([gain_one, gain_two], [offset_one, offset_two, offset_mix, offset_down], head_part, hidden_part)

    def spread_out(values, shape):
        lead = shape[:-1]
        values = values.reshape(lead + (shards, shape[-1]))
        return jnp.moveaxis(values, -2, 0).reshape(shards, -1)

    gain_sums = jnp.stack([jnp.stack(entry[0]) for entry in vectors])
    offset_sums = jnp.stack([jnp.stack(entry[1]) for entry in vectors])
    head_sums = jnp.stack([entry[2] for entry in vectors])
    hidden_sums = jnp.stack([entry[3] for entry in vectors])
    vector_pack = jnp.concatenate(
        [spread_out(values, part.shape) for values, part in zip((gain_sums, offset_sums, head_sums, hidden_sums), small_parts)]
        + [jnp.zeros((shards, small_padded - small_total), FULL)], axis=1)
    vector_pack = lax.all_to_all(vector_pack.reshape(shards, -1, 128), "shard", 0, 0)
    vector_own = context_sum(jnp.sum(vector_pack, axis=0)).reshape(-1)
    vector_out = []
    for index, part in enumerate(small_parts):
        start = sum(small_sizes[:index])
        vector_out.append(vector_own[start:start + small_sizes[index]].reshape(part.shape))
    gains_grad, offsets_grad, head_grad, hidden_grad = vector_out

    feed_own = [context_sum(share) for share in feed_shares]
    attend_own = [context_sum(share) for share in attend_shares]
    projection_grad = jnp.stack(
        [jnp.stack([share[:, k * head_cols:(k + 1) * head_cols] for k in range(3)]) for share in attend_own])
    mixing_grad = jnp.stack([share[:, 3 * head_cols:].T for share in attend_own])
    expansion_grad = jnp.stack([share[:, :hidden] for share in feed_own])
    contraction_grad = jnp.stack([share[:, hidden:].T for share in feed_own])
    return (
        stream.reshape(rows, block, width),
        upstream.reshape(rows, block, width),
        projection_grad,
        head_grad,
        mixing_grad,
        expansion_grad,
        hidden_grad,
        contraction_grad,
        gains_grad,
        offsets_grad,
    )


def solution(mesh):
    in_specs = (
        P("shard", "context", None),
        P("shard", "context"),
        P(None, None, "shard", "tensor"),
        P(None, None, "tensor", "shard"),
        P(None, "tensor", "shard"),
        P(None, "shard", "tensor"),
        P(None, "tensor", "shard"),
        P(None, "tensor", "shard"),
        P(None, None, "shard"),
        P(None, None, "shard"),
        P("shard", "context", None),
    )
    out_specs = (
        P("shard", "context", None),
        P("shard", "context", None),
        P(None, None, "shard", "tensor"),
        P(None, None, "tensor", "shard"),
        P(None, "tensor", "shard"),
        P(None, "shard", "tensor"),
        P(None, "tensor", "shard"),
        P(None, "tensor", "shard"),
        P(None, None, "shard"),
        P(None, None, "shard"),
    )
    return jax.shard_map(
        per_device, mesh=mesh, in_specs=in_specs, out_specs=out_specs, check_vma=False
    )
```

time: 1540 us -> 627 us (0.41)
  waiting for transfers between devices: 913 us -> 322 us
  blocking collectives: 372 us -> 0 us
  starting transfers between devices: 1.58 us -> 76.4 us
  matrix products: 92.7 us -> 68.4 us
  local copies, waits for them, and re-layouts: 100 us -> 82.9 us
    all_gather x15 -> x0, blocking collectives: 297 us -> none  [the longest x2 48.7 us: per_device(): lax.all_gather(offsets[layer_index], 'shard', axis=1, tiled=True)]
    reduce_scatter x8 -> x4, waiting for transfers between devices: 385 us -> 176 us  [scatter(): return lax.psum_scatter(packed, 'shard', scatter_dimension=0, tiled=True)]
    psum x10 -> x0, waiting for transfers between devices: 181 us -> none  [the longest x2 44.5 us: per_device(): lax.psum(feed_partial.astype(jnp.bfloat16), 'tensor').astype(jnp.float32)]
    unnamed x30 -> x6, waiting for transfers between devices: 165 us -> 0.71 us
    all_gather x6 -> x2, waiting for transfers between devices: 181 us -> 49.1 us  [per_device(): gathered.append(lax.all_gather(packed, 'shard', axis=0, tiled=True))]
    ppermute x0 -> x33, waiting for transfers between devices: none -> 81.6 us  [the longest x4 29.2 us: from_after(): lax.ppermute(block, 'context', [(i + steps, i) for i in range(size - step...]
    unnamed x1 -> x0, blocking collectives: 75.6 us -> none
    ppermute x0 -> x33, starting transfers between devices: none -> 62.6 us  [the longest x15 31.4 us: context_sum(): lax.ppermute(part, 'context', [(i, (i + steps) % size) for i in range(siz...]
  transfers between devices with their start and end apart: 27 -> 41, of which waited for: 20 -> 27; matrix products, arithmetic and copies ran while one was open for 9% -> 19% of each run, Pallas kernels for 0% -> 0%
where the time goes in v1:
time: 627 us; the launch traced here: 617 us
  waiting for transfers between devices  322 us (51%)
  local copies, waits for them, and re-layouts  82.9 us (13%)
  starting transfers between devices  76.4 us (12%)
  matrix products  68.4 us (11%)
  other arithmetic  50.4 us (8%)
  between operations  16.4 us (3%)
    reduce_scatter x4, waiting for transfers between devices, scatter(): return lax.psum_scatter(packed, 'shard', scatter_dimension=0, tiled=True)  176 us
    all_gather x2, waiting for transfers between devices, per_device(): gathered.append(lax.all_gather(packed, 'shard', axis=0, tiled=True))  49.1 us
    dot_general x24, matrix products, dot(): lax.dot_general(left, right, (((left_dim,), (right_dim,)), ((), ())), pre...  46.1 us
    ppermute x15, starting transfers between devices, context_sum(): lax.ppermute(part, 'context', [(i, (i + steps) % size) for i in range(siz...  31.4 us
    ppermute x4, waiting for transfers between devices, from_after(): lax.ppermute(block, 'context', [(i + steps, i) for i in range(size - step...  29.2 us
    ppermute x15, waiting for transfers between devices, context_sum(): lax.ppermute(part, 'context', [(i, (i + steps) % size) for i in range(siz...  25.6 us
    ppermute x6, waiting for transfers between devices, from_before(): lax.ppermute(block, 'context', [(i, i + steps) for i in range(size - step...  24.7 us
    ppermute x6, starting transfers between devices, from_before(): lax.ppermute(block, 'context', [(i, i + steps) for i in range(size - step...  24.6 us
  transfers between devices with their start and end apart: 41, of which 27 were waited for; matrix products, arithmetic and copies ran while one was open for 19% of the time, Pallas kernels for 0%

profile of v1, /device:TPU:0, one launch (start us, length us, event | category | flops | bytes accessed | tf_op | source)
XLA Modules:
  0.0 616.9 jit_solution(8124101954752828164)
XLA Ops:
  14.1 5.2 collective-permute-start.2
  19.3 2.6 collective-permute-start.3
  23.3 7.9 %all-to-all-start = ((bf16[16,8,128]{2,1,0:T(8,128)(2,1)}), bf16[16,8,128]{2,1,0:T(8,128)(2,1)S(1)}, u32[]{:S(2)}, u32[]{:S(2)}) async-start(bf16[16,8,128]{2,1,0:T(8,128)(2,1)} %broadcast_in_dim.34), calls=%async_computation | async-start | bytes 65536 | tf_op jit(solution)/shard_map/all_to_all | solution.py:118
  31.7 7.1 %all-to-all-done = bf16[16,8,128]{2,1,0:T(8,128)(2,1)S(1)} async-done(((bf16[16,8,128]{2,1,0:T(8,128)(2,1)}), bf16[16,8,128]{2,1,0:T(8,128)(2,1)S(1)}, u32[]{:S(2)}, u32[]{:S(2)}) %all-to-all-start) | async-done | bytes 32800 | tf_op jit(solution)/shard_map/all_to_all | solution.py:118
  42.3 39.0 %all-gather.3.cloned.1.call-done = bf16[768,4608]{1,0:T(8,128)(2,1)} async-done(((bf16[48,4608]{1,0:T(8,128)(2,1)}), bf16[768,4608]{1,0:T(8,128)(2,1)}) %all-gather.3.cloned.1.call-update) | async-done | bytes 7077904 | tf_op jit(solution)/shard_map/all_gather | solution.py:111
  83.5 4.9 collective-permute-start
  88.4 2.5 collective-permute-start.1
  91.4 6.5 %collective-permute-done = bf16[2,128,768]{2,1,0:T(8,128)(2,1)S(1)} collective-permute-done((bf16[2,128,768]{2,1,0:T(8,128)(2,1)S(1)}, bf16[2,128,768]{2,1,0:T(8,128)(2,1)S(1)}, u32[]{:S(2)}, u32[]{:S(2)}) %collective-permute-start) | collective-permute-done | bytes 393248 | tf_op jit(solution)/shard_map/ppermute | solution.py:56
  98.0 7.3 %collective-permute-done.1 = bf16[2,128,768]{2,1,0:T(8,128)(2,1)S(1)} collective-permute-done((bf16[2,128,768]{2,1,0:T(8,128)(2,1)S(1)}, bf16[2,128,768]{2,1,0:T(8,128)(2,1)S(1)}, u32[]{:S(2)}, u32[]{:S(2)}) %collective-permute-start.1) | collective-permute-done | bytes 393248 | tf_op jit(solution)/shard_map/ppermute | solution.py:56
  126.0 2.6 convolution_add_fusion.3
  128.6 4.2 fusion.15
  138.5 10.1 %all-gather.5.cloned.1.call-done = bf16[768,4608]{1,0:T(8,128)(2,1)} async-done(((bf16[48,4608]{1,0:T(8,128)(2,1)}), bf16[768,4608]{1,0:T(8,128)(2,1)}) %all-gather.5.cloned.1.call-update) | async-done | bytes 7077904 | tf_op jit(solution)/shard_map/all_gather | solution.py:111
  148.6 2.5 fusion.3
  151.9 5.7 collective-permute-start.6
  157.6 3.7 collective-permute-start.7
  163.1 3.6 collective-permute-done.6
  166.7 7.3 %collective-permute-done.7 = bf16[2,128,768]{2,1,0:T(8,128)(2,1)} collective-permute-done((bf16[2,128,768]{2,1,0:T(8,128)(2,1)}, bf16[2,128,768]{2,1,0:T(8,128)(2,1)}, u32[]{:S(2)}, u32[]{:S(2)}) %collective-permute-start.7) | collective-permute-done | bytes 393248 | tf_op jit(solution)/shard_map/ppermute | solution.py:56
  184.6 2.6 fusion.49
  200.9 2.7 convolution_add_fusion.2
  203.6 4.2 fusion.135
  212.2 2.5 multiply_reduce_fusion
  214.8 3.5 fusion.119
  223.5 3.4 fusion.80
  228.8 2.7 copy.186
  231.5 2.6 fusion.100
  234.2 2.7 copy.185
  246.2 7.9 %collective-permute-done.11 = bf16[2,128,768]{2,1,0:T(8,128)(2,1)} collective-permute-done((bf16[2,128,768]{2,1,0:T(8,128)(2,1)}, bf16[2,128,768]{2,1,0:T(8,128)(2,1)}, u32[]{:S(2)}, u32[]{:S(2)}) %collective-permute-start.11) | collective-permute-done | bytes 393248 | tf_op jit(solution)/shard_map/ppermute | solution.py:61
  254.0 3.1 collective-permute-done.12
  282.6 2.7 copy.195
  298.5 15.0 %collective-permute-done.15 = bf16[2,128,768]{2,1,0:T(8,128)(2,1)} collective-permute-done((bf16[2,128,768]{2,1,0:T(8,128)(2,1)}, bf16[2,128,768]{2,1,0:T(8,128)(2,1)}, u32[]{:S(2)}, u32[]{:S(2)}) %collective-permute-start.15) | collective-permute-done | bytes 393248 | tf_op jit(solution)/shard_map/ppermute | solution.py:61
  313.5 3.2 collective-permute-done.16
  325.4 2.7 pad_maximum_fusion.1
  332.4 2.7 pad_maximum_fusion
  352.5 5.2 all-to-all-start.1
  357.7 7.6 %all-to-all-done.1 = f32[16,8,128]{2,1,0:T(8,128)S(1)} async-done(((f32[16,8,128]{2,1,0:T(8,128)}), f32[16,8,128]{2,1,0:T(8,128)S(1)}, u32[]{:S(2)}, u32[]{:S(2)}) %all-to-all-start.1) | async-done | bytes 65568 | tf_op jit(solution)/shard_map/all_to_all | solution.py:254
  365.4 7.0 %collective-permute-start.24 = (f32[8,128]{1,0:T(8,128)S(1)}, f32[8,128]{1,0:T(8,128)S(1)}, u32[]{:S(2)}, u32[]{:S(2)}) collective-permute-start(f32[8,128]{1,0:T(8,128)S(1)} %reduce_sum.395), channel_id=1, source_target_pairs={{0,2},{2,4},{4,6},{6,0},{1,3},{3,5},{5,7},{7,1},{8,10},{10,12},{12... | collective-permute-start | bytes 12296 | tf_op jit(solution)/shard_map/ppermute | solution.py:68
  372.4 2.8 collective-permute-start.26
  377.8 3.8 collective-permute-start.22
  388.0 41.1 %reduce-scatter.5.cloned.1.call-done = bf16[48,1536]{1,0:T(8,128)(2,1)} async-done(((bf16[768,1536]{1,0:T(8,128)(2,1)}), bf16[48,1536]{1,0:T(8,128)(2,1)}) %reduce-scatter.5.cloned.1.call-update) | async-done | bytes 147472 | tf_op jit(solution)/shard_map/reduce_scatter | solution.py:182
  430.5 2.7 collective-permute-start.19
  439.6 70.2 %reduce-scatter.11.cloned.1.call-done = bf16[48,3072]{1,0:T(8,128)(2,1)} async-done(((bf16[768,3072]{1,0:T(8,128)(2,1)}), bf16[48,3072]{1,0:T(8,128)(2,1)}) %reduce-scatter.11.cloned.1.call-update) | async-done | bytes 294928 | tf_op jit(solution)/shard_map/reduce_scatter | solution.py:182
  511.3 2.7 collective-permute-start.31
  517.1 3.1 collective-permute-done.30
  520.2 5.6 collective-permute-done.31
  525.9 64.9 %reduce-scatter.9.cloned.1.call-done = bf16[48,3072]{1,0:T(8,128)(2,1)} async-done(((bf16[768,3072]{1,0:T(8,128)(2,1)}), bf16[48,3072]{1,0:T(8,128)(2,1)}) %reduce-scatter.9.cloned.1.call-update) | async-done | bytes 294928 | tf_op jit(solution)/shard_map/reduce_scatter | solution.py:182
  592.4 2.7 collective-permute-start.28
  596.5 4.7 collective-permute-done.27
  601.2 5.6 collective-permute-done.28
  (514 shorter events, 183.8 us)
Async XLA Ops:
  7.2 24.0 %copy-start.2 = (f32[2,128,768]{2,1,0:T(8,128)S(1)}, f32[2,128,768]{2,1,0:T(8,128)}, u32[]{:S(2)}) copy-start(f32[2,128,768]{2,1,0:T(8,128)} %param.11) | copy-start | bytes 2359300
  7.2 74.0 %all-gather.3.cloned.1.call-start = ((), (), s32[]{:S(2)}) async-start(), calls=%async_computation.6 | async-start | bytes 7520256 | tf_op jit(solution)/shard_map/all_gather | solution.py:111
  13.4 135.2 %all-gather.5.cloned.1.call-start = ((), (), s32[]{:S(2)}) async-start(), calls=%async_computation.7 | async-start | bytes 7520256 | tf_op jit(solution)/shard_map/all_gather | solution.py:111
  14.1 76.8 %collective-permute-start.2 = (s32[2,128]{1,0:T(2,128)S(1)}, s32[2,128]{1,0:T(2,128)S(1)}, u32[]{:S(2)}, u32[]{:S(2)}) collective-permute-start(s32[2,128]{1,0:T(2,128)S(1)} %copy-done.105), channel_id=1, source_target_pairs={{0,4},{2,6},{1,5},{3,7},{8,12},{10,14},{9,13},{11,15},{16,20},{18,... | collective-permute-start | bytes 3080 | tf_op jit(solution)/shard_map/ppermute | solution.py:56
  19.3 71.7 %collective-permute-start.3 = (s32[2,128]{1,0:T(2,128)S(1)}, s32[2,128]{1,0:T(2,128)S(1)}, u32[]{:S(2)}, u32[]{:S(2)}) collective-permute-start(s32[2,128]{1,0:T(2,128)S(1)} %copy-done.105), channel_id=1, source_target_pairs={{0,2},{2,4},{4,6},{1,3},{3,5},{5,7},{8,10},{10,12},{12,14},{9,11},... | collective-permute-start | bytes 3080 | tf_op jit(solution)/shard_map/ppermute | solution.py:56
  23.3 15.6 %all-to-all-start = ((bf16[16,8,128]{2,1,0:T(8,128)(2,1)}), bf16[16,8,128]{2,1,0:T(8,128)(2,1)S(1)}, u32[]{:S(2)}, u32[]{:S(2)}) async-start(bf16[16,8,128]{2,1,0:T(8,128)(2,1)} %broadcast_in_dim.34), calls=%async_computation | async-start | bytes 65536 | tf_op jit(solution)/shard_map/all_to_all | solution.py:118
  31.2 346.5 %reduce-scatter.7.cloned.1.call-start = ((), (), s32[]{:S(2)}) async-start(), calls=%async_computation.9 | async-start | bytes 2506752 | tf_op jit(solution)/shard_map/reduce_scatter | solution.py:182
  31.4 52.0 %copy-start.80 = (f32[256]{0:T(256)}, f32[256]{0:T(256)S(1)}, u32[]{:S(2)}) copy-start(f32[256]{0:T(256)S(1)} %get-tuple-element.151) | copy-start | bytes 3076
  31.7 51.7 %copy-start.82 = (f32[256]{0:T(256)}, f32[256]{0:T(256)S(1)}, u32[]{:S(2)}) copy-start(f32[256]{0:T(256)S(1)} %rsqrt_bitcast_fusion) | copy-start | bytes 3076
  40.8 42.6 %copy-start.58 = (f32[768]{0:T(1024)}, f32[768]{0:T(1024)S(1)}, u32[]{:S(2)}) copy-start(f32[768]{0:T(1024)S(1)} %mul.315) | copy-start | bytes 9220
  42.3 39.0 %copy-start.42 = (bf16[256,768]{1,0:T(8,128)(2,1)}, bf16[256,768]{1,0:T(8,128)(2,1)S(1)}, u32[]{:S(2)}) copy-start(bf16[256,768]{1,0:T(8,128)(2,1)S(1)} %add_convert_fusion.3) | copy-start | bytes 1179652
  83.5 14.5 %collective-permute-start = (bf16[2,128,768]{2,1,0:T(8,128)(2,1)S(1)}, bf16[2,128,768]{2,1,0:T(8,128)(2,1)S(1)}, u32[]{:S(2)}, u32[]{:S(2)}) collective-permute-start(bf16[2,128,768]{2,1,0:T(8,128)(2,1)S(1)} %bitcast.247), channel_id=1, source_target_pairs={{0,4},{2,6},{1,5},{3,7},{8,12},{10,14},{9,13},{11,15},{16,20},{18,... | collective-permute-start | bytes 1179656 | tf_op jit(solution)/shard_map/ppermute | solution.py:56
  88.4 16.8 %collective-permute-start.1 = (bf16[2,128,768]{2,1,0:T(8,128)(2,1)S(1)}, bf16[2,128,768]{2,1,0:T(8,128)(2,1)S(1)}, u32[]{:S(2)}, u32[]{:S(2)}) collective-permute-start(bf16[2,128,768]{2,1,0:T(8,128)(2,1)S(1)} %bitcast.248), channel_id=1, source_target_pairs={{0,2},{2,4},{4,6},{1,3},{3,5},{5,7},{8,10},{10,12},{12,14},{9,11},... | collective-permute-start | bytes 1179656 | tf_op jit(solution)/shard_map/ppermute | solution.py:56
  114.4 8.5 %collective-permute-start.4 = (f32[256,768]{1,0:T(8,128)}, f32[256,768]{1,0:T(8,128)}, u32[]{:S(2)}, u32[]{:S(2)}) collective-permute-start(f32[256,768]{1,0:T(8,128)} %fusion.74), channel_id=1, source_target_pairs={{0,1},{1,0},{2,3},{3,2},{4,5},{5,4},{6,7},{7,6},{8,9},{9,8},{10,11... | collective-permute-start | bytes 2359304 | tf_op jit(solution)/shard_map/ppermute | solution.py:50
  132.9 2.7 collective-permute-start.5
  151.9 14.8 %collective-permute-start.6 = (bf16[2,128,768]{2,1,0:T(8,128)(2,1)}, bf16[2,128,768]{2,1,0:T(8,128)(2,1)}, u32[]{:S(2)}, u32[]{:S(2)}) collective-permute-start(bf16[2,128,768]{2,1,0:T(8,128)(2,1)} %bitcast.30), channel_id=1, source_target_pairs={{0,4},{2,6},{1,5},{3,7},{8,12},{10,14},{9,13},{11,15},{16,20},{18,... | collective-permute-start | bytes 1179656 | tf_op jit(solution)/shard_map/ppermute | solution.py:56
  157.6 16.4 %collective-permute-start.7 = (bf16[2,128,768]{2,1,0:T(8,128)(2,1)}, bf16[2,128,768]{2,1,0:T(8,128)(2,1)}, u32[]{:S(2)}, u32[]{:S(2)}) collective-permute-start(bf16[2,128,768]{2,1,0:T(8,128)(2,1)} %bitcast.30), channel_id=1, source_target_pairs={{0,2},{2,4},{4,6},{1,3},{3,5},{5,7},{8,10},{10,12},{12,14},{9,11},... | collective-permute-start | bytes 1179656 | tf_op jit(solution)/shard_map/ppermute | solution.py:56
  189.9 8.8 %collective-permute-start.8 = (f32[256,768]{1,0:T(8,128)}, f32[256,768]{1,0:T(8,128)}, u32[]{:S(2)}, u32[]{:S(2)}) collective-permute-start(f32[256,768]{1,0:T(8,128)} %fusion.71), channel_id=1, source_target_pairs={{0,1},{1,0},{2,3},{3,2},{4,5},{5,4},{6,7},{7,6},{8,9},{9,8},{10,11... | collective-permute-start | bytes 2359304 | tf_op jit(solution)/shard_map/ppermute | solution.py:50
  209.5 2.7 collective-permute-start.10
  211.9 2.8 collective-permute-start.9
  239.6 14.5 %collective-permute-start.11 = (bf16[2,128,768]{2,1,0:T(8,128)(2,1)}, bf16[2,128,768]{2,1,0:T(8,128)(2,1)}, u32[]{:S(2)}, u32[]{:S(2)}) collective-permute-start(bf16[2,128,768]{2,1,0:T(8,128)(2,1)} %get-tuple-element.106), channel_id=1, source_target_pairs={{2,0},{4,2},{6,4},{3,1},{5,3},{7,5},{10,8},{12,10},{14,12},{11,9},... | collective-permute-start | bytes 1179656 | tf_op jit(solution)/shard_map/ppermute | solution.py:61
  240.9 16.2 %collective-permute-start.12 = (bf16[2,128,768]{2,1,0:T(8,128)(2,1)}, bf16[2,128,768]{2,1,0:T(8,128)(2,1)}, u32[]{:S(2)}, u32[]{:S(2)}) collective-permute-start(bf16[2,128,768]{2,1,0:T(8,128)(2,1)} %get-tuple-element.107), channel_id=1, source_target_pairs={{4,0},{6,2},{5,1},{7,3},{12,8},{14,10},{13,9},{15,11},{20,16},{22,... | collective-permute-start | bytes 1179656 | tf_op jit(solution)/shard_map/ppermute | solution.py:61
  262.0 2.0 collective-permute-start.13
  270.0 2.1 collective-permute-start.14
  271.6 157.4 %reduce-scatter.5.cloned.1.call-start = ((), (), s32[]{:S(2)}) async-start(), calls=%async_computation.8 | async-start | bytes 2506752 | tf_op jit(solution)/shard_map/reduce_scatter | solution.py:182
  293.5 20.0 %collective-permute-start.15 = (bf16[2,128,768]{2,1,0:T(8,128)(2,1)}, bf16[2,128,768]{2,1,0:T(8,128)(2,1)}, u32[]{:S(2)}, u32[]{:S(2)}) collective-permute-start(bf16[2,128,768]{2,1,0:T(8,128)(2,1)} %get-tuple-element.104), channel_id=1, source_target_pairs={{2,0},{4,2},{6,4},{3,1},{5,3},{7,5},{10,8},{12,10},{14,12},{11,9},... | collective-permute-start | bytes 1179656 | tf_op jit(solution)/shard_map/ppermute | solution.py:61
  294.8 21.9 %collective-permute-start.16 = (bf16[2,128,768]{2,1,0:T(8,128)(2,1)}, bf16[2,128,768]{2,1,0:T(8,128)(2,1)}, u32[]{:S(2)}, u32[]{:S(2)}) collective-permute-start(bf16[2,128,768]{2,1,0:T(8,128)(2,1)} %get-tuple-element.105), channel_id=1, source_target_pairs={{4,0},{6,2},{5,1},{7,3},{12,8},{14,10},{13,9},{15,11},{20,16},{22,... | collective-permute-start | bytes 1179656 | tf_op jit(solution)/shard_map/ppermute | solution.py:61
  298.0 20.9 %copy-start.48 = (bf16[256,384]{1,0:T(8,128)(2,1)}, bf16[256,384]{1,0:T(8,128)(2,1)S(1)}, u32[]{:S(2)}) copy-start(bf16[256,384]{1,0:T(8,128)(2,1)S(1)} %copy.196) | copy-start | bytes 589828
  321.2 188.6 %reduce-scatter.11.cloned.1.call-start = ((), (), s32[]{:S(2)}) async-start(), calls=%async_computation.11 | async-start | bytes 5013504 | tf_op jit(solution)/shard_map/reduce_scatter | solution.py:182
  328.1 262.7 %reduce-scatter.9.cloned.1.call-start = ((), (), s32[]{:S(2)}) async-start(), calls=%async_computation.10 | async-start | bytes 5013504 | tf_op jit(solution)/shard_map/reduce_scatter | solution.py:182
  343.3 6.8 %collective-permute-start.17 = (bf16[256,768]{1,0:T(8,128)(2,1)S(1)}, bf16[256,768]{1,0:T(8,128)(2,1)S(1)}, u32[]{:S(2)}, u32[]{:S(2)}) collective-permute-start(bf16[256,768]{1,0:T(8,128)(2,1)S(1)} %fusion.36), channel_id=1, source_target_pairs={{0,1},{1,0},{2,3},{3,2},{4,5},{5,4},{6,7},{7,6},{8,9},{9,8},{10,11... | collective-permute-start | bytes 1179656 | tf_op jit(solution)/shard_map/ppermute | solution.py:50
  348.9 26.3 %copy-start.83 = (f32[256]{0:T(256)S(1)}, f32[256]{0:T(256)}, u32[]{:S(2)}) copy-start(f32[256]{0:T(256)} %copy-done.82) | copy-start | bytes 3076
  352.5 12.9 %all-to-all-start.1 = ((f32[16,8,128]{2,1,0:T(8,128)}), f32[16,8,128]{2,1,0:T(8,128)S(1)}, u32[]{:S(2)}, u32[]{:S(2)}) async-start(f32[16,8,128]{2,1,0:T(8,128)} %bitcast.123), calls=%async_computation.3 | async-start | bytes 131072 | tf_op jit(solution)/shard_map/all_to_all | solution.py:254
  365.4 11.0 %collective-permute-start.24 = (f32[8,128]{1,0:T(8,128)S(1)}, f32[8,128]{1,0:T(8,128)S(1)}, u32[]{:S(2)}, u32[]{:S(2)}) collective-permute-start(f32[8,128]{1,0:T(8,128)S(1)} %reduce_sum.395), channel_id=1, source_target_pairs={{0,2},{2,4},{4,6},{6,0},{1,3},{3,5},{5,7},{7,1},{8,10},{10,12},{12... | collective-permute-start | bytes 12296 | tf_op jit(solution)/shard_map/ppermute | solution.py:68
  372.4 5.1 collective-permute-start.25
  372.4 5.1 collective-permute-start.26
  377.7 7.7 %collective-permute-start.21 = (bf16[48,1536]{1,0:T(8,128)(2,1)}, bf16[48,1536]{1,0:T(8,128)(2,1)S(1)}, u32[]{:S(2)}, u32[]{:S(2)}) collective-permute-start(bf16[48,1536]{1,0:T(8,128)(2,1)} %reduce-scatter.7.cloned.1.call-done), channel_id=1, source_target_pairs={{0,2},{2,4},{4,6},{6,0},{1,3},{3,5},{5,7},{7,1},{8,10},{10,12},{12... | collective-permute-start | bytes 442376 | tf_op jit(solution)/shard_map/ppermute | solution.py:68
  377.8 8.8 %collective-permute-start.22 = (bf16[48,1536]{1,0:T(8,128)(2,1)}, bf16[48,1536]{1,0:T(8,128)(2,1)S(1)}, u32[]{:S(2)}, u32[]{:S(2)}) collective-permute-start(bf16[48,1536]{1,0:T(8,128)(2,1)} %reduce-scatter.7.cloned.1.call-done), channel_id=1, source_target_pairs={{0,4},{2,6},{4,0},{6,2},{1,5},{3,7},{5,1},{7,3},{8,12},{10,14},{12... | collective-permute-start | bytes 442376 | tf_op jit(solution)/shard_map/ppermute | solution.py:68
  381.6 5.4 collective-permute-start.23
  429.1 7.9 %collective-permute-start.18 = (bf16[48,1536]{1,0:T(8,128)(2,1)}, bf16[48,1536]{1,0:T(8,128)(2,1)S(1)}, u32[]{:S(2)}, u32[]{:S(2)}) collective-permute-start(bf16[48,1536]{1,0:T(8,128)(2,1)} %reduce-scatter.5.cloned.1.call-done), channel_id=1, source_target_pairs={{0,2},{2,4},{4,6},{6,0},{1,3},{3,5},{5,7},{7,1},{8,10},{10,12},{12... | collective-permute-start | bytes 442376 | tf_op jit(solution)/shard_map/ppermute | solution.py:68
  430.5 8.0 %collective-permute-start.19 = (bf16[48,1536]{1,0:T(8,128)(2,1)}, bf16[48,1536]{1,0:T(8,128)(2,1)S(1)}, u32[]{:S(2)}, u32[]{:S(2)}) collective-permute-start(bf16[48,1536]{1,0:T(8,128)(2,1)} %reduce-scatter.5.cloned.1.call-done), channel_id=1, source_target_pairs={{0,4},{2,6},{4,0},{6,2},{1,5},{3,7},{5,1},{7,3},{8,12},{10,14},{12... | collective-permute-start | bytes 442376 | tf_op jit(solution)/shard_map/ppermute | solution.py:68
  433.3 5.4 collective-permute-start.20
  509.8 10.3 %collective-permute-start.30 = (bf16[48,3072]{1,0:T(8,128)(2,1)}, bf16[48,3072]{1,0:T(8,128)(2,1)S(1)}, u32[]{:S(2)}, u32[]{:S(2)}) collective-permute-start(bf16[48,3072]{1,0:T(8,128)(2,1)} %reduce-scatter.11.cloned.1.call-done), channel_id=1, source_target_pairs={{0,2},{2,4},{4,6},{6,0},{1,3},{3,5},{5,7},{7,1},{8,10},{10,12},{12... | collective-permute-start | bytes 884744 | tf_op jit(solution)/shard_map/ppermute | solution.py:68
  511.3 14.4 %collective-permute-start.31 = (bf16[48,3072]{1,0:T(8,128)(2,1)}, bf16[48,3072]{1,0:T(8,128)(2,1)S(1)}, u32[]{:S(2)}, u32[]{:S(2)}) collective-permute-start(bf16[48,3072]{1,0:T(8,128)(2,1)} %reduce-scatter.11.cloned.1.call-done), channel_id=1, source_target_pairs={{0,4},{2,6},{4,0},{6,2},{1,5},{3,7},{5,1},{7,3},{8,12},{10,14},{12... | collective-permute-start | bytes 884744 | tf_op jit(solution)/shard_map/ppermute | solution.py:68
  514.0 11.7 %collective-permute-start.32 = (bf16[48,3072]{1,0:T(8,128)(2,1)}, bf16[48,3072]{1,0:T(8,128)(2,1)S(1)}, u32[]{:S(2)}, u32[]{:S(2)}) collective-permute-start(bf16[48,3072]{1,0:T(8,128)(2,1)} %reduce-scatter.11.cloned.1.call-done), channel_id=1, source_target_pairs={{0,6},{2,0},{4,2},{6,4},{1,7},{3,1},{5,3},{7,5},{8,14},{10,8},{12,... | collective-permute-start | bytes 884744 | tf_op jit(solution)/shard_map/ppermute | solution.py:68
  590.8 10.3 %collective-permute-start.27 = (bf16[48,3072]{1,0:T(8,128)(2,1)}, bf16[48,3072]{1,0:T(8,128)(2,1)S(1)}, u32[]{:S(2)}, u32[]{:S(2)}) collective-permute-start(bf16[48,3072]{1,0:T(8,128)(2,1)} %reduce-scatter.9.cloned.1.call-done), channel_id=1, source_target_pairs={{0,2},{2,4},{4,6},{6,0},{1,3},{3,5},{5,7},{7,1},{8,10},{10,12},{12... | collective-permute-start | bytes 884744 | tf_op jit(solution)/shard_map/ppermute | solution.py:68
  592.4 14.4 %collective-permute-start.28 = (bf16[48,3072]{1,0:T(8,128)(2,1)}, bf16[48,3072]{1,0:T(8,128)(2,1)S(1)}, u32[]{:S(2)}, u32[]{:S(2)}) collective-permute-start(bf16[48,3072]{1,0:T(8,128)(2,1)} %reduce-scatter.9.cloned.1.call-done), channel_id=1, source_target_pairs={{0,4},{2,6},{4,0},{6,2},{1,5},{3,7},{5,1},{7,3},{8,12},{10,14},{12... | collective-permute-start | bytes 884744 | tf_op jit(solution)/shard_map/ppermute | solution.py:68
  595.0 11.7 %collective-permute-start.29 = (bf16[48,3072]{1,0:T(8,128)(2,1)}, bf16[48,3072]{1,0:T(8,128)(2,1)S(1)}, u32[]{:S(2)}, u32[]{:S(2)}) collective-permute-start(bf16[48,3072]{1,0:T(8,128)(2,1)} %reduce-scatter.9.cloned.1.call-done), channel_id=1, source_target_pairs={{0,6},{2,0},{4,2},{6,4},{1,7},{3,1},{5,3},{7,5},{8,14},{10,8},{12,... | collective-permute-start | bytes 884744 | tf_op jit(solution)/shard_map/ppermute | solution.py:68
  (112 other events, 574.6 us)
Sparse Core Ops, SparseCore 0:
  13.5 67.7 all-gather.2
  83.9 64.6 all-gather.4
  271.7 79.8 reduce-scatter.6
  354.8 74.2 reduce-scatter.4
  432.3 77.5 reduce-scatter.10
  513.0 77.7 reduce-scatter.8
